TPU v7x, 256 devices: a whole 4x4x8 slice. The times are simulated.
256 devices in a mesh: section: 4 (over x), expert: 32 (over z, y_lo, core), dp: 2 (over y_hi).
Axes of the slice: x: 4, y: 4 (y_hi: 2, y_lo: 2; y = y_hi * 2 + y_lo), z: 8, core: 2. Of those that a mesh axis runs over, the one named last changes fastest.
Arguments:
- fwd_in: bfloat16 [4, 3072, 2048], P('section', 'expert'), may hold values from -6 to 6
- fwd_routes: int32 [4, 3072, 8], P('section', 'expert'), may hold values from 0 to 31, all different within a row; in each aligned block of 96 rows (0 to 95, 96 to 191, ..., all dimensions but the last counted through in order) at most 26 rows name the same one
- fwd_numer: int32 [4, 3072, 8], P('section', 'expert'), may hold values from 1 to 255
- bwd_saved: bfloat16 [4, 3072, 2048], P('section', 'expert'), may hold values from -6 to 6
- bwd_routes: int32 [4, 3072, 8], P('section', 'expert'), may hold values from 0 to 31, all different within a row; in each aligned block of 96 rows (0 to 95, 96 to 191, ..., all dimensions but the last counted through in order) at most 26 rows name the same one
- bwd_numer: int32 [4, 3072, 8], P('section', 'expert'), may hold values from 1 to 255
- bwd_grad: bfloat16 [4, 3072, 2048], P('section', 'expert'), may hold values from -6 to 6
- w_gate: bfloat16 [4, 32, 2048, 768], P('section', 'expert', None, 'dp'), may hold values from -0.125 to 0.125
- w_up: bfloat16 [4, 32, 2048, 768], P('section', 'expert', None, 'dp'), may hold values from -0.125 to 0.125
- w_down: bfloat16 [4, 32, 768, 2048], P('section', 'expert', 'dp'), may hold values from -0.21875 to 0.21875
Outputs:
- next_fwd: bfloat16 [4, 3072, 2048], P('section', 'expert')
- next_bwd: bfloat16 [4, 3072, 2048], P('section', 'expert')
- grad_gate: bfloat16 [4, 32, 2048, 768], P('section', 'expert', None, 'dp')
- grad_up: bfloat16 [4, 32, 2048, 768], P('section', 'expert', None, 'dp')
- grad_down: bfloat16 [4, 32, 768, 2048], P('section', 'expert', 'dp')
Inputs may be any that keep to these rules, and one draw needn't show every extreme that they name: `fwd_routes`: each token names 8 different experts. In each aligned block of 96 rows (the tokens of one index of expert of one section) no expert is named more than 26 times; in some blocks some expert is named exactly 26 times. `bwd_routes`: each token names 8 different experts. In each aligned block of 96 rows (the tokens of one index of expert of one section) no expert is named more than 26 times; in some blocks some expert is named exactly 26 times.
All inputs are finite; a program needn't handle non-finite values.
Results may differ from a plain program's by a relative error of at most 0.0058.
Values may be sent and summed in bfloat16 or wider, within the bound.
A program may use at most 128 MiB of HBM per device.

v0:
```python
import jax
import jax.numpy as jnp
from jax import lax
from jax.sharding import PartitionSpec as P

EXPERTS = 32
MOST = 26


def passed_along(block, axis, distance):
    devices = range(lax.axis_size(axis))
    route = [((i - distance) % len(devices), i) for i in devices]
    return lax.ppermute(block, axis, route)


def swapped(block):
    return lax.ppermute(block, "dp", [(0, 1), (1, 0)])


def slot_ranks(routes):
    flat_routes = routes.reshape(-1)
    onehot_table = (flat_routes[:, None] == jnp.arange(EXPERTS, dtype=jnp.int32)[None, :]).astype(
        jnp.int32
    )
    earlier = jnp.cumsum(onehot_table, 0) - onehot_table
    return (flat_routes, jnp.sum(earlier * onehot_table, 1))


def combine_weights(numerators):
    counted = numerators.astype(jnp.float32)
    return counted / jnp.sum(counted, -1, keepdims=True)


def packed_rows(rows, positions, groups):
    filled = jnp.zeros((EXPERTS * MOST, rows.shape[-1]), rows.dtype).at[positions].set(rows)
    return filled.reshape(groups, EXPERTS // groups, MOST, rows.shape[-1])


def handoff(value, direction):
    return passed_along(value, "section", direction)


def project(rows, gate_weight, up_weight):
    gate_value = jnp.einsum("semd,edf->semf", rows, gate_weight, preferred_element_type=jnp.float32)
    up_value = jnp.einsum("semd,edf->semf", rows, up_weight, preferred_element_type=jnp.float32)
    return (gate_value, up_value)


def local_backward(gate_value, up_value, grad_rows, down_weight):
    silu_gate = jax.nn.silu(gate_value)
    sigmoid_gate = jax.nn.sigmoid(gate_value)
    hidden = (silu_gate * up_value).astype(jnp.bfloat16)
    hidden_grad = jnp.einsum(
        "semd,efd->semf", grad_rows, down_weight, preferred_element_type=jnp.float32
    )
    up_grad = (hidden_grad * silu_gate).astype(jnp.bfloat16)
    gate_grad = (
        hidden_grad * up_value * sigmoid_gate * (1.0 + gate_value * (1.0 - sigmoid_gate))
    ).astype(jnp.bfloat16)
    return (hidden, gate_grad, up_grad)


def weight_terms(saved_rows, grad_rows, back_hidden, gate_grad, up_grad):
    gate_term = jnp.einsum(
        "semd,semf->edf", saved_rows, gate_grad, preferred_element_type=jnp.float32
    )
    up_term = jnp.einsum("semd,semf->edf", saved_rows, up_grad, preferred_element_type=jnp.float32)
    down_term = jnp.einsum(
        "semf,semd->efd", back_hidden, grad_rows, preferred_element_type=jnp.float32
    )
    return (gate_term, up_term, down_term)


def mix_rows(base, returned, positions, weights, choices_per):
    width = returned.shape[-1]
    picked = (
        returned.reshape(-1, width)[positions].reshape(-1, choices_per, width).astype(jnp.float32)
    )
    return (base.astype(jnp.float32) + jnp.sum(weights[:, :, None] * picked, 1)).astype(
        jnp.bfloat16
    )


def local(
    fwd_in, fwd_routes, fwd_numer, bwd_saved, bwd_routes, bwd_numer, bwd_grad, w_gate, w_up, w_down
):
    groups = lax.axis_size("expert")
    inputs = fwd_in[0]
    saved = bwd_saved[0]
    grad_in = bwd_grad[0]
    model_width = inputs.shape[-1]
    half = model_width // lax.axis_size("dp")
    mine = lax.axis_index("dp") * half
    theirs = half - mine
    choices_per = fwd_routes.shape[-1]
    gate_half = w_gate[0]
    up_half = w_up[0]
    down_half = w_down[0]
    down_recv, gate_recv, up_recv = swapped(
        (
            lax.dynamic_slice_in_dim(down_half, theirs, half, 2),
            lax.dynamic_slice_in_dim(gate_half, theirs, half, 1),
            lax.dynamic_slice_in_dim(up_half, theirs, half, 1),
        )
    )
    down_mine = jnp.concatenate([lax.dynamic_slice_in_dim(down_half, mine, half, 2), down_recv], 1)
    gate_mine = jnp.concatenate([lax.dynamic_slice_in_dim(gate_half, mine, half, 1), gate_recv], 2)
    up_mine = jnp.concatenate([lax.dynamic_slice_in_dim(up_half, mine, half, 1), up_recv], 2)
    fwd_flat, fwd_rank = slot_ranks(fwd_routes[0])
    back_flat, back_rank = slot_ranks(bwd_routes[0])
    fwd_positions = fwd_flat * MOST + fwd_rank
    back_positions = back_flat * MOST + back_rank
    mixing = combine_weights(fwd_numer[0])
    back_mixing = combine_weights(bwd_numer[0])
    unit_weights = jnp.ones_like(back_mixing)
    scaled_grad = (back_mixing[:, :, None] * grad_in.astype(jnp.float32)[:, None, :]).astype(
        jnp.bfloat16
    )
    send_inputs = packed_rows(jnp.repeat(inputs, choices_per, 0), fwd_positions, groups)
    send_saved = packed_rows(jnp.repeat(saved, choices_per, 0), back_positions, groups)
    send_grad = packed_rows(scaled_grad.reshape(-1, model_width), back_positions, groups)
    recv_inputs = lax.all_to_all(send_inputs, "expert", split_axis=0, concat_axis=0, tiled=True)
    recv_saved = lax.all_to_all(send_saved, "expert", split_axis=0, concat_axis=0, tiled=True)
    recv_grad = lax.all_to_all(send_grad, "expert", split_axis=0, concat_axis=0, tiled=True)
    gate_value, up_value = project(recv_inputs, gate_half, up_half)
    hidden = (jax.nn.silu(gate_value) * up_value).astype(jnp.bfloat16)
    hidden_all = jnp.concatenate([hidden, swapped(hidden)], -1)
    out_part = jnp.einsum(
        "semf,efd->semd", hidden_all, down_mine, preferred_element_type=jnp.float32
    ).astype(jnp.bfloat16)
    back_gate, back_up = project(recv_saved, gate_half, up_half)
    back_hidden, gate_grad, up_grad = local_backward(back_gate, back_up, recv_grad, down_half)
    gate_term, up_term, down_term = weight_terms(
        recv_saved, recv_grad, back_hidden, gate_grad, up_grad
    )
    gate_other, up_other = swapped((gate_grad, up_grad))
    gate_all = jnp.concatenate([gate_grad, gate_other], -1)
    up_all = jnp.concatenate([up_grad, up_other], -1)
    grad_part = (
        jnp.einsum("semf,edf->semd", gate_all, gate_mine, preferred_element_type=jnp.float32)
        + jnp.einsum("semf,edf->semd", up_all, up_mine, preferred_element_type=jnp.float32)
    ).astype(jnp.bfloat16)
    back_out = lax.all_to_all(out_part, "expert", split_axis=0, concat_axis=0, tiled=True)
    back_grad = lax.all_to_all(grad_part, "expert", split_axis=0, concat_axis=0, tiled=True)
    inputs_part = lax.dynamic_slice_in_dim(inputs, mine, half, 1)
    grad_in_part = lax.dynamic_slice_in_dim(grad_in, mine, half, 1)
    layer_out = mix_rows(inputs_part, back_out, fwd_positions, mixing, choices_per)
    input_grad = mix_rows(grad_in_part, back_grad, back_positions, unit_weights, choices_per)
    layer_out = lax.all_gather(layer_out, "dp", axis=1, tiled=True)
    input_grad = lax.all_gather(input_grad, "dp", axis=1, tiled=True)
    next_fwd = handoff(layer_out[None], 1)
    next_bwd = handoff(input_grad[None], -1)
    gate_sum = gate_term.astype(jnp.bfloat16)
    up_sum = up_term.astype(jnp.bfloat16)
    down_sum = down_term.astype(jnp.bfloat16)
    return (next_fwd, next_bwd, gate_sum[None], up_sum[None], down_sum[None])


def solution(mesh):
    in_specs = (
        P("section", "expert", None),
        P("section", "expert", None),
        P("section", "expert", None),
        P("section", "expert", None),
        P("section", "expert", None),
        P("section", "expert", None),
        P("section", "expert", None),
        P("section", "expert", None, "dp"),
        P("section", "expert", None, "dp"),
        P("section", "expert", "dp", None),
    )
    out_specs = (
        P("section", "expert", None),
        P("section", "expert", None),
        P("section", "expert", None, "dp"),
        P("section", "expert", None, "dp"),
        P("section", "expert", "dp", None),
    )
    return jax.shard_map(local, mesh=mesh, in_specs=in_specs, out_specs=out_specs, check_vma=False)
```

profile of v0, /device:TPU:8, one launch (start us, length us, event | category | flops | bytes accessed | tf_op | source)
XLA Modules:
  0.0 513.9 jit_solution(12449324526280599132)
XLA Ops:
  10.6 12.6 %scatter_custom_fusion.1 = bf16[832,2048]{1,0:T(8,128)(2,1)} fusion(s32[768]{0:T(1024)S(1)} %get-tuple-element.15, f32[96,2048]{1,0:T(8,128)S(1)} %bitcast_convert_fusion.3, f32[768]{0:T(1024)S(1)} %div.39, bf16[]{:T(256)} %constant.36.clone.1), kind=kCustom, calls=%fused_computation.24 | custom fusion | flops 3145728 | bytes 4198402 | tf_op jit(solution)/shard_map/scatter | solution.py:35
  23.2 4.8 reshape.280
  28.1 10.5 %all-to-all-start.2 = ((bf16[32,1,26,2048]{3,2,1,0:T(8,128)(2,1)}), bf16[32,1,26,2048]{3,2,1,0:T(8,128)(2,1)}, u32[]{:S(2)}, u32[]{:S(2)}) async-start(bf16[32,1,26,2048]{3,2,1,0:T(8,128)(2,1)} %bitcast.269), calls=%async_computation.2 | async-start | bytes 8388608 | tf_op jit(solution)/shard_map/all_to_all | solution.py:124
  38.6 9.0 %scatter_custom_fusion.2 = bf16[832,2048]{1,0:T(8,128)(2,1)} fusion(s32[768]{0:T(1024)S(1)} %get-tuple-element.15, bf16[]{:T(256)} %constant.36.clone.1, bf16[96,2048]{1,0:T(8,128)(2,1)S(1)} %bitcast.266), kind=kCustom, calls=%fused_computation.31 | custom fusion | bytes 3801090 | tf_op jit(solution)/shard_map/scatter | solution.py:35
  47.6 4.9 reshape.284
  52.5 79.9 %all-to-all-done.2 = bf16[32,1,26,2048]{3,2,1,0:T(8,128)(2,1)} async-done(((bf16[32,1,26,2048]{3,2,1,0:T(8,128)(2,1)}), bf16[32,1,26,2048]{3,2,1,0:T(8,128)(2,1)}, u32[]{:S(2)}, u32[]{:S(2)}) %all-to-all-start.2) | async-done | bytes 3407904 | tf_op jit(solution)/shard_map/all_to_all | solution.py:124
  132.5 7.5 %all-to-all-start.3 = ((bf16[32,1,26,2048]{3,2,1,0:T(8,128)(2,1)}), bf16[32,1,26,2048]{3,2,1,0:T(8,128)(2,1)}, u32[]{:S(2)}, u32[]{:S(2)}) async-start(bf16[32,1,26,2048]{3,2,1,0:T(8,128)(2,1)} %bitcast.268), calls=%async_computation.3 | async-start | bytes 8388608 | tf_op jit(solution)/shard_map/all_to_all | solution.py:123
  140.0 8.9 %scatter_custom_fusion = bf16[832,2048]{1,0:T(8,128)(2,1)} fusion(s32[768]{0:T(1024)S(1)} %get-tuple-element.14, bf16[]{:T(256)} %constant.36.clone.1, bf16[96,2048]{1,0:T(8,128)(2,1)S(1)} %bitcast.270), kind=kCustom, calls=%fused_computation.33 | custom fusion | bytes 3801090 | tf_op jit(solution)/shard_map/scatter | solution.py:35
  148.9 4.9 reshape.272
  153.8 80.2 %all-to-all-done.3 = bf16[32,1,26,2048]{3,2,1,0:T(8,128)(2,1)} async-done(((bf16[32,1,26,2048]{3,2,1,0:T(8,128)(2,1)}), bf16[32,1,26,2048]{3,2,1,0:T(8,128)(2,1)}, u32[]{:S(2)}, u32[]{:S(2)}) %all-to-all-start.3) | async-done | bytes 3407904 | tf_op jit(solution)/shard_map/all_to_all | solution.py:123
  234.1 7.6 %all-to-all-start = ((bf16[32,1,26,2048]{3,2,1,0:T(8,128)(2,1)}), bf16[32,1,26,2048]{3,2,1,0:T(8,128)(2,1)}, u32[]{:S(2)}, u32[]{:S(2)}) async-start(bf16[32,1,26,2048]{3,2,1,0:T(8,128)(2,1)} %bitcast.267), calls=%async_computation | async-start | bytes 8388608 | tf_op jit(solution)/shard_map/all_to_all | solution.py:122
  244.4 4.2 fusion.79
  248.7 4.8 fusion.74
  253.5 5.7 %multiply_convert_fusion.2 = (bf16[32,1,26,384]{3,0,2,1:T(8,128)(2,1)S(1)}, bf16[32,1,26,384]{3,0,2,1:T(8,128)(2,1)S(1)}, f32[32,1,26,384]{3,0,2,1:T(8,128)}) fusion(f32[32,1,26,384]{3,0,2,1:T(8,128)S(1)} %fusion.74, f32[32,1,26,384]{3,0,2,1:T(8,128)S(1)} %fusion.79, bf16[1,1,2048,384]{3,2,1,0:T(8,128)(2,1)S(1)} %copy-done.4, ...), kind=kOutput, calls=%fused_computation.85 | convolution fusion | flops 1312776192 | bytes 10092544 | tf_op jit(solution)/shard_map/semd,edf->semf/dot_general | solution.py:44
  264.2 21.9 %collective-permute-done.5 = bf16[1,1024,384]{2,1,0:T(8,128)(2,1)S(1)} collective-permute-done((bf16[1,1024,384]{2,1,0:T(8,128)(2,1)S(1)}, bf16[1,1024,384]{2,1,0:T(8,128)(2,1)S(1)}, u32[]{:S(2)}, u32[]{:S(2)}) %collective-permute-start.5) | collective-permute-done | bytes 786464 | tf_op jit(solution)/shard_map/ppermute | solution.py:17
  286.2 21.0 %collective-permute-done.6 = bf16[32,1,26,384]{3,0,2,1:T(8,128)(2,1)S(1)} collective-permute-done((bf16[32,1,26,384]{3,0,2,1:T(8,128)(2,1)S(1)}, bf16[32,1,26,384]{3,0,2,1:T(8,128)(2,1)S(1)}, u32[]{:S(2)}, u32[]{:S(2)}) %collective-permute-start.6) | collective-permute-done | bytes 639008 | tf_op jit(solution)/shard_map/ppermute | solution.py:17
  308.7 29.1 %collective-permute-done.3 = bf16[1,1024,384]{2,1,0:T(8,128)(2,1)S(1)} collective-permute-done((bf16[1,1024,384]{2,1,0:T(8,128)(2,1)S(1)}, bf16[1,1024,384]{2,1,0:T(8,128)(2,1)S(1)}, u32[]{:S(2)}, u32[]{:S(2)}) %collective-permute-start.3) | collective-permute-done | bytes 786464 | tf_op jit(solution)/shard_map/ppermute | solution.py:17
  337.8 13.2 %collective-permute-done.4 = bf16[32,1,26,384]{3,0,2,1:T(8,128)(2,1)S(1)} collective-permute-done((bf16[32,1,26,384]{3,0,2,1:T(8,128)(2,1)S(1)}, bf16[32,1,26,384]{3,0,2,1:T(8,128)(2,1)S(1)}, u32[]{:S(2)}, u32[]{:S(2)}) %collective-permute-start.4) | collective-permute-done | bytes 639008 | tf_op jit(solution)/shard_map/ppermute | solution.py:17
  354.8 8.4 %all-to-all-start.4 = ((bf16[32,1,26,1024]{3,2,1,0:T(8,128)(2,1)}), bf16[32,1,26,1024]{3,2,1,0:T(8,128)(2,1)S(1)}, u32[]{:S(2)}, u32[]{:S(2)}) async-start(bf16[32,1,26,1024]{3,2,1,0:T(8,128)(2,1)} %copy.48), calls=%async_computation.4 | async-start | bytes 4194304 | tf_op jit(solution)/shard_map/all_to_all | solution.py:144
  366.2 4.3 fusion.64
  370.5 4.5 fusion.94
  377.4 25.5 %collective-permute-done = bf16[1,384,1024]{2,1,0:T(8,128)(2,1)S(1)} collective-permute-done((bf16[1,384,1024]{2,1,0:T(8,128)(2,1)S(1)}, bf16[1,384,1024]{2,1,0:T(8,128)(2,1)S(1)}, u32[]{:S(2)}, u32[]{:S(2)}) %collective-permute-start) | collective-permute-done | bytes 786464 | tf_op jit(solution)/shard_map/ppermute | solution.py:17
  402.8 16.6 %collective-permute-done.1 = bf16[32,1,26,384]{3,0,2,1:T(8,128)(2,1)S(1)} collective-permute-done((bf16[32,1,26,384]{3,0,2,1:T(8,128)(2,1)S(1)}, bf16[32,1,26,384]{3,0,2,1:T(8,128)(2,1)S(1)}, u32[]{:S(2)}, u32[]{:S(2)}) %collective-permute-start.1) | collective-permute-done | bytes 639008 | tf_op jit(solution)/shard_map/ppermute | solution.py:17
  424.7 8.0 %all-to-all-start.1 = ((bf16[32,1,26,1024]{3,2,1,0:T(8,128)(2,1)}), bf16[32,1,26,1024]{3,2,1,0:T(8,128)(2,1)}, u32[]{:S(2)}, u32[]{:S(2)}) async-start(bf16[32,1,26,1024]{3,2,1,0:T(8,128)(2,1)} %copy.38), calls=%async_computation.1 | async-start | bytes 4194304 | tf_op jit(solution)/shard_map/all_to_all | solution.py:143
  432.9 6.8 %fusion.36 = bf16[1,1,2048,384]{3,2,1,0:T(8,128)(2,1)} fusion(bf16[32,1,26,2048]{3,2,1,0:T(8,128)(2,1)} %all-to-all-done.3, bf16[32,1,26,384]{3,0,2,1:T(8,128)(2,1)} %copy-done.13), kind=kOutput, calls=%fused_computation.41 | convolution fusion | flops 1309409280 | bytes 5619712 | tf_op jit(solution)/shard_map/semd,semf->edf/dot_general | solution.py:64
  439.6 6.5 %fusion.42 = bf16[1,1,384,2048]{3,2,1,0:T(8,128)(2,1)} fusion(bf16[32,1,26,2048]{3,2,1,0:T(8,128)(2,1)} %all-to-all-done.2, f32[32,1,26,384]{3,0,2,1:T(8,128)S(1)} %copy-done.15, f32[32,1,26,384]{3,0,2,1:T(8,128)S(1)} %copy-done.16), kind=kOutput, calls=%fused_computation.43 | convolution fusion | flops 1311326208 | bytes 7536640 | tf_op jit(solution)/shard_map/semf,semd->efd/dot_general | solution.py:68
  448.7 3.6 gather_fusion.1
  454.7 13.6 %all_gather.7 = bf16[96,2048]{1,0:T(8,128)(2,1)S(1)} all-gather(bf16[96,1024]{1,0:T(8,128)(2,1)S(1)} %fusion.114), channel_id=1, replica_groups=mesh['section'=4,'expert'=32,'dp'=2] {'dp'}, dimensions={1}, use_global_device_ids=true | all-gather | bytes 589824 | tf_op jit(solution)/shard_map/all_gather | solution.py:150
  471.1 11.7 %all-to-all-done.1 = bf16[32,1,26,1024]{3,2,1,0:T(8,128)(2,1)} async-done(((bf16[32,1,26,1024]{3,2,1,0:T(8,128)(2,1)}), bf16[32,1,26,1024]{3,2,1,0:T(8,128)(2,1)}, u32[]{:S(2)}, u32[]{:S(2)}) %all-to-all-start.1) | async-done | bytes 1703968 | tf_op jit(solution)/shard_map/all_to_all | solution.py:143
  485.3 3.6 gather_fusion
  491.4 9.1 %all_gather.6 = bf16[96,2048]{1,0:T(8,128)(2,1)S(1)} all-gather(bf16[96,1024]{1,0:T(8,128)(2,1)S(1)} %fusion.115), channel_id=1, replica_groups=mesh['section'=4,'expert'=32,'dp'=2] {'dp'}, dimensions={1}, use_global_device_ids=true | all-gather | bytes 589824 | tf_op jit(solution)/shard_map/all_gather | solution.py:149
  502.2 6.5 %fusion.39 = bf16[1,1,2048,384]{3,2,1,0:T(8,128)(2,1)} fusion(bf16[32,1,26,2048]{3,2,1,0:T(8,128)(2,1)} %all-to-all-done.3, bf16[32,1,26,384]{3,0,2,1:T(8,128)(2,1)S(1)} %copy-done.12), kind=kOutput, calls=%fused_computation.42 | convolution fusion | flops 1309409280 | bytes 5619712 | tf_op jit(solution)/shard_map/semd,semf->edf/dot_general | solution.py:67
  (98 shorter events, 53.2 us)
Async XLA Ops:
  0.6 37.9 %copy-start = (bf16[1,96,2048]{2,1,0:T(8,128)(2,1)S(1)}, bf16[1,96,2048]{2,1,0:T(8,128)(2,1)}, u32[]{:S(2)}) copy-start(bf16[1,96,2048]{2,1,0:T(8,128)(2,1)} %param.13) | copy-start | bytes 1179652
  0.6 9.6 %copy-start.9 = (bf16[1,96,2048]{2,1,0:T(8,128)(2,1)S(1)}, bf16[1,96,2048]{2,1,0:T(8,128)(2,1)}, u32[]{:S(2)}) copy-start(bf16[1,96,2048]{2,1,0:T(8,128)(2,1)} %param.16) | copy-start | bytes 1179652
  28.1 104.4 %all-to-all-start.2 = ((bf16[32,1,26,2048]{3,2,1,0:T(8,128)(2,1)}), bf16[32,1,26,2048]{3,2,1,0:T(8,128)(2,1)}, u32[]{:S(2)}, u32[]{:S(2)}) async-start(bf16[32,1,26,2048]{3,2,1,0:T(8,128)(2,1)} %bitcast.269), calls=%async_computation.2 | async-start | bytes 8388608 | tf_op jit(solution)/shard_map/all_to_all | solution.py:124
  132.5 7.5 %copy-start.8 = (bf16[1,96,2048]{2,1,0:T(8,128)(2,1)S(1)}, bf16[1,96,2048]{2,1,0:T(8,128)(2,1)}, u32[]{:S(2)}) copy-start(bf16[1,96,2048]{2,1,0:T(8,128)(2,1)} %param.10) | copy-start | bytes 1179652
  132.5 101.6 %all-to-all-start.3 = ((bf16[32,1,26,2048]{3,2,1,0:T(8,128)(2,1)}), bf16[32,1,26,2048]{3,2,1,0:T(8,128)(2,1)}, u32[]{:S(2)}, u32[]{:S(2)}) async-start(bf16[32,1,26,2048]{3,2,1,0:T(8,128)(2,1)} %bitcast.268), calls=%async_computation.3 | async-start | bytes 8388608 | tf_op jit(solution)/shard_map/all_to_all | solution.py:123
  234.1 7.6 %copy-start.6 = (bf16[1,1,2048,384]{3,2,1,0:T(8,128)(2,1)S(1)}, bf16[1,1,2048,384]{3,2,1,0:T(8,128)(2,1)}, u32[]{:S(2)}) copy-start(bf16[1,1,2048,384]{3,2,1,0:T(8,128)(2,1)} %param.18) | copy-start | bytes 4718596
  234.1 120.8 %all-to-all-start = ((bf16[32,1,26,2048]{3,2,1,0:T(8,128)(2,1)}), bf16[32,1,26,2048]{3,2,1,0:T(8,128)(2,1)}, u32[]{:S(2)}, u32[]{:S(2)}) async-start(bf16[32,1,26,2048]{3,2,1,0:T(8,128)(2,1)} %bitcast.267), calls=%async_computation | async-start | bytes 8388608 | tf_op jit(solution)/shard_map/all_to_all | solution.py:122
  241.8 6.8 %copy-start.3 = (bf16[1,1,384,2048]{3,2,1,0:T(8,128)(2,1)S(1)}, bf16[1,1,384,2048]{3,2,1,0:T(8,128)(2,1)}, u32[]{:S(2)}) copy-start(bf16[1,1,384,2048]{3,2,1,0:T(8,128)(2,1)} %param.19) | copy-start | bytes 4718596
  241.8 44.3 %collective-permute-start.5 = (bf16[1,1024,384]{2,1,0:T(8,128)(2,1)S(1)}, bf16[1,1024,384]{2,1,0:T(8,128)(2,1)S(1)}, u32[]{:S(2)}, u32[]{:S(2)}) collective-permute-start(bf16[1,1024,384]{2,1,0:T(8,128)(2,1)S(1)} %get-tuple-element.10), channel_id=1, source_target_pairs={{0,1},{1,0},{2,3},{3,2},{4,5},{5,4},{6,7},{7,6},{8,9},{9,8},{10,11... | collective-permute-start | bytes 2359304 | tf_op jit(solution)/shard_map/ppermute | solution.py:17
  248.7 4.8 copy-start.14
  248.7 4.8 copy-start.4
  259.2 49.5 %copy-start.11 = (bf16[32,1,26,384]{3,0,2,1:T(8,128)(2,1)}, bf16[32,1,26,384]{3,0,2,1:T(8,128)(2,1)S(1)}, u32[]{:S(2)}) copy-start(bf16[32,1,26,384]{3,0,2,1:T(8,128)(2,1)S(1)} %get-tuple-element.6) | copy-start | bytes 1916932
  259.2 91.8 %copy-start.13 = (bf16[32,1,26,384]{3,0,2,1:T(8,128)(2,1)}, bf16[32,1,26,384]{3,0,2,1:T(8,128)(2,1)S(1)}, u32[]{:S(2)}) copy-start(bf16[32,1,26,384]{3,0,2,1:T(8,128)(2,1)S(1)} %get-tuple-element.5) | copy-start | bytes 1916932
  259.2 47.9 %collective-permute-start.6 = (bf16[32,1,26,384]{3,0,2,1:T(8,128)(2,1)S(1)}, bf16[32,1,26,384]{3,0,2,1:T(8,128)(2,1)S(1)}, u32[]{:S(2)}, u32[]{:S(2)}) collective-permute-start(bf16[32,1,26,384]{3,0,2,1:T(8,128)(2,1)S(1)} %get-tuple-element.6), channel_id=1, source_target_pairs={{0,1},{1,0},{2,3},{3,2},{4,5},{5,4},{6,7},{7,6},{8,9},{9,8},{10,11... | collective-permute-start | bytes 1916936 | tf_op jit(solution)/shard_map/ppermute | solution.py:17
  260.6 77.2 %collective-permute-start.3 = (bf16[1,1024,384]{2,1,0:T(8,128)(2,1)S(1)}, bf16[1,1024,384]{2,1,0:T(8,128)(2,1)S(1)}, u32[]{:S(2)}, u32[]{:S(2)}) collective-permute-start(bf16[1,1024,384]{2,1,0:T(8,128)(2,1)S(1)} %get-tuple-element.8), channel_id=1, source_target_pairs={{0,1},{1,0},{2,3},{3,2},{4,5},{5,4},{6,7},{7,6},{8,9},{9,8},{10,11... | collective-permute-start | bytes 2359304 | tf_op jit(solution)/shard_map/ppermute | solution.py:17
  263.0 88.0 %collective-permute-start.4 = (bf16[32,1,26,384]{3,0,2,1:T(8,128)(2,1)S(1)}, bf16[32,1,26,384]{3,0,2,1:T(8,128)(2,1)S(1)}, u32[]{:S(2)}, u32[]{:S(2)}) collective-permute-start(bf16[32,1,26,384]{3,0,2,1:T(8,128)(2,1)S(1)} %get-tuple-element.5), channel_id=1, source_target_pairs={{0,1},{1,0},{2,3},{3,2},{4,5},{5,4},{6,7},{7,6},{8,9},{9,8},{10,11... | collective-permute-start | bytes 1916936 | tf_op jit(solution)/shard_map/ppermute | solution.py:17
  354.8 68.4 %all-to-all-start.4 = ((bf16[32,1,26,1024]{3,2,1,0:T(8,128)(2,1)}), bf16[32,1,26,1024]{3,2,1,0:T(8,128)(2,1)S(1)}, u32[]{:S(2)}, u32[]{:S(2)}) async-start(bf16[32,1,26,1024]{3,2,1,0:T(8,128)(2,1)} %copy.48), calls=%async_computation.4 | async-start | bytes 4194304 | tf_op jit(solution)/shard_map/all_to_all | solution.py:144
  363.2 3.0 copy-start.5
  364.9 5.6 %copy-start.7 = (bf16[1,1,2048,384]{3,2,1,0:T(8,128)(2,1)S(1)}, bf16[1,1,2048,384]{3,2,1,0:T(8,128)(2,1)}, u32[]{:S(2)}) copy-start(bf16[1,1,2048,384]{3,2,1,0:T(8,128)(2,1)} %param.18) | copy-start | bytes 4718596
  364.9 38.0 %collective-permute-start = (bf16[1,384,1024]{2,1,0:T(8,128)(2,1)S(1)}, bf16[1,384,1024]{2,1,0:T(8,128)(2,1)S(1)}, u32[]{:S(2)}, u32[]{:S(2)}) collective-permute-start(bf16[1,384,1024]{2,1,0:T(8,128)(2,1)S(1)} %get-tuple-element.12), channel_id=1, source_target_pairs={{0,1},{1,0},{2,3},{3,2},{4,5},{5,4},{6,7},{7,6},{8,9},{9,8},{10,11... | collective-permute-start | bytes 2359304 | tf_op jit(solution)/shard_map/ppermute | solution.py:17
  370.5 6.9 %copy-start.10 = (s32[1,96,8]{1,2,0:T(8,128)S(1)}, s32[1,96,8]{1,2,0:T(8,128)}, u32[]{:S(2)}) copy-start(s32[1,96,8]{1,2,0:T(8,128)} %param.12) | copy-start | bytes 9220
  375.0 44.5 %collective-permute-start.1 = (bf16[32,1,26,384]{3,0,2,1:T(8,128)(2,1)S(1)}, bf16[32,1,26,384]{3,0,2,1:T(8,128)(2,1)S(1)}, u32[]{:S(2)}, u32[]{:S(2)}) collective-permute-start(bf16[32,1,26,384]{3,0,2,1:T(8,128)(2,1)S(1)} %fusion.94), channel_id=1, source_target_pairs={{0,1},{1,0},{2,3},{3,2},{4,5},{5,4},{6,7},{7,6},{8,9},{9,8},{10,11... | collective-permute-start | bytes 1916936 | tf_op jit(solution)/shard_map/ppermute | solution.py:17
  423.3 1.4 copy-start.2
  424.7 58.2 %all-to-all-start.1 = ((bf16[32,1,26,1024]{3,2,1,0:T(8,128)(2,1)}), bf16[32,1,26,1024]{3,2,1,0:T(8,128)(2,1)}, u32[]{:S(2)}, u32[]{:S(2)}) async-start(bf16[32,1,26,1024]{3,2,1,0:T(8,128)(2,1)} %copy.38), calls=%async_computation.1 | async-start | bytes 4194304 | tf_op jit(solution)/shard_map/all_to_all | solution.py:143
  432.8 6.8 %copy-start.15 = (f32[32,1,26,384]{3,0,2,1:T(8,128)S(1)}, f32[32,1,26,384]{3,0,2,1:T(8,128)}, u32[]{:S(2)}) copy-start(f32[32,1,26,384]{3,0,2,1:T(8,128)} %copy-done.14) | copy-start | bytes 3833860
  432.8 6.8 %copy-start.16 = (f32[32,1,26,384]{3,0,2,1:T(8,128)S(1)}, f32[32,1,26,384]{3,0,2,1:T(8,128)}, u32[]{:S(2)}) copy-start(f32[32,1,26,384]{3,0,2,1:T(8,128)} %get-tuple-element.13) | copy-start | bytes 3833860
  468.4 40.4 %collective-permute-start.7 = (bf16[1,96,2048]{2,1,0:T(8,128)(2,1)S(1)}, bf16[1,96,2048]{2,1,0:T(8,128)(2,1)S(1)}, u32[]{:S(2)}, u32[]{:S(2)}) collective-permute-start(bf16[1,96,2048]{2,1,0:T(8,128)(2,1)S(1)} %bitcast.271), channel_id=1, source_target_pairs={{64,0},{128,64},{192,128},{0,192},{65,1},{129,65},{193,129},{1,193... | collective-permute-start | bytes 1179656 | tf_op jit(solution)/shard_map/ppermute | solution.py:13
  488.9 13.3 %copy-start.12 = (bf16[32,1,26,384]{3,0,2,1:T(8,128)(2,1)S(1)}, bf16[32,1,26,384]{3,0,2,1:T(8,128)(2,1)}, u32[]{:S(2)}) copy-start(bf16[32,1,26,384]{3,0,2,1:T(8,128)(2,1)} %copy-done.11) | copy-start | bytes 1916932
  500.5 11.6 %collective-permute-start.2 = (bf16[1,96,2048]{2,1,0:T(8,128)(2,1)S(1)}, bf16[1,96,2048]{2,1,0:T(8,128)(2,1)S(1)}, u32[]{:S(2)}, u32[]{:S(2)}) collective-permute-start(bf16[1,96,2048]{2,1,0:T(8,128)(2,1)S(1)} %bitcast.272), channel_id=1, source_target_pairs={{192,0},{0,64},{64,128},{128,192},{193,1},{1,65},{65,129},{129,193... | collective-permute-start | bytes 1179656 | tf_op jit(solution)/shard_map/ppermute | solution.py:13
  502.2 11.5 %copy-start.1 = (bf16[1,96,2048]{2,1,0:T(8,128)(2,1)S(1)}, bf16[1,96,2048]{2,1,0:T(8,128)(2,1)}, u32[]{:S(2)}) copy-start(bf16[1,96,2048]{2,1,0:T(8,128)(2,1)} %param.13) | copy-start | bytes 1179652
where the time goes:
time: 521 us; the launch traced here: 514 us
  waiting for transfers between devices  303 us (58%)
  local copies, waits for them, and re-layouts  57.6 us (11%)
  starting transfers between devices  57.5 us (11%)
  matrix products  47.8 us (9%)
  other arithmetic  24.4 us (5%)
  blocking collectives  22.7 us (4%)
    ppermute x6, waiting for transfers between devices, swapped(): return lax.ppermute(block, 'dp', [(0, 1), (1, 0)])  127 us
    all_to_all x1, waiting for transfers between devices, local(): lax.all_to_all(send_saved, 'expert', split_axis=0, concat_axis=0, tiled=T...  80.2 us
    all_to_all x1, waiting for transfers between devices, local(): lax.all_to_all(send_grad, 'expert', split_axis=0, concat_axis=0, tiled=True)  79.9 us
    scatter x2, local copies, waits for them, and re-layouts, packed_rows(): jnp.zeros((EXPERTS * MOST, rows.shape[-1]), rows.dtype).at[positions]  18 us
    reshape x3, local copies, waits for them, and re-layouts, packed_rows(): return filled.reshape(groups, EXPERTS // groups, MOST, rows.shape[-1])  14.6 us
    all_gather x1, blocking collectives, local(): input_grad = lax.all_gather(input_grad, 'dp', axis=1, tiled=True)  13.6 us
    scatter x1, other arithmetic, packed_rows(): jnp.zeros((EXPERTS * MOST, rows.shape[-1]), rows.dtype).at[positions]  12.6 us
    all_to_all x1, waiting for transfers between devices, local(): lax.all_to_all(out_part, 'expert', split_axis=0, concat_axis=0, tiled=True)  11.7 us
  transfers between devices with their start and end apart: 13, of which 10 were waited for; matrix products, arithmetic and copies ran while one was open for 19% of the time, Pallas kernels for 0%

commit v1 on v0

--- a/solution.py
+++ b/solution.py
@@ -146,8 +146,12 @@
     grad_in_part = lax.dynamic_slice_in_dim(grad_in, mine, half, 1)
     layer_out = mix_rows(inputs_part, back_out, fwd_positions, mixing, choices_per)
     input_grad = mix_rows(grad_in_part, back_grad, back_positions, unit_weights, choices_per)
-    layer_out = lax.all_gather(layer_out, "dp", axis=1, tiled=True)
-    input_grad = lax.all_gather(input_grad, "dp", axis=1, tiled=True)
+    fix_floor = lambda x_local, load: jnp.split(
+        jax.lax.all_gather(jnp.concatenate([x_local, load], 0), "dp", axis=1, tiled=True),
+        [x_local.shape[0]],
+        0,
+    )
+    layer_out, input_grad = fix_floor(layer_out, input_grad)
     next_fwd = handoff(layer_out[None], 1)
     next_bwd = handoff(input_grad[None], -1)
     gate_sum = gate_term.astype(jnp.bfloat16)

time: 521 us -> 528 us (1.013)
  waiting for transfers between devices: 303 us -> 320 us
  blocking collectives: 22.7 us -> 13.4 us
    all_to_all x1, waiting for transfers between devices: 11.7 us -> 28 us  [local(): lax.all_to_all(out_part, 'expert', split_axis=0, concat_axis=0, tiled=True)]
    all_gather x2 -> x1, blocking collectives: 22.7 us -> 13.4 us  [local(): jax.lax.all_gather(jnp.concatenate([x_local, load], 0), 'dp', axis=1, til...]
  transfers between devices with their start and end apart: 13 -> 13, of which waited for: 10 -> 11; matrix products, arithmetic and copies ran while one was open for 19% -> 17% of each run, Pallas kernels for 0% -> 0%
where the time goes in v1:
time: 528 us; the launch traced here: 521 us
  waiting for transfers between devices  320 us (61%)
  local copies, waits for them, and re-layouts  57.6 us (11%)
  starting transfers between devices  56.1 us (11%)
  matrix products  47.8 us (9%)
  other arithmetic  24.4 us (5%)
  blocking collectives  13.4 us (3%)
    ppermute x6, waiting for transfers between devices, swapped(): return lax.ppermute(block, 'dp', [(0, 1), (1, 0)])  127 us
    all_to_all x1, waiting for transfers between devices, local(): lax.all_to_all(send_saved, 'expert', split_axis=0, concat_axis=0, tiled=T...  80.2 us
    all_to_all x1, waiting for transfers between devices, local(): lax.all_to_all(send_grad, 'expert', split_axis=0, concat_axis=0, tiled=True)  80 us
    all_to_all x1, waiting for transfers between devices, local(): lax.all_to_all(out_part, 'expert', split_axis=0, concat_axis=0, tiled=True)  28 us
    scatter x2, local copies, waits for them, and re-layouts, packed_rows(): jnp.zeros((EXPERTS * MOST, rows.shape[-1]), rows.dtype).at[positions]  17.9 us
    reshape x3, local copies, waits for them, and re-layouts, packed_rows(): return filled.reshape(groups, EXPERTS // groups, MOST, rows.shape[-1])  14.6 us
    all_gather x1, blocking collectives, local(): jax.lax.all_gather(jnp.concatenate([x_local, load], 0), 'dp', axis=1, til...  13.4 us
    scatter x1, other arithmetic, packed_rows(): jnp.zeros((EXPERTS * MOST, rows.shape[-1]), rows.dtype).at[positions]  12.6 us
  transfers between devices with their start and end apart: 13, of which 11 were waited for; matrix products, arithmetic and copies ran while one was open for 17% of the time, Pallas kernels for 0%

profile of v1, /device:TPU:8, one launch (start us, length us, event | category | flops | bytes accessed | tf_op | source)
XLA Modules:
  0.0 520.8 jit_solution(2970456714837771382)
XLA Ops:
  10.6 12.6 %scatter_custom_fusion.1 = bf16[832,2048]{1,0:T(8,128)(2,1)} fusion(s32[768]{0:T(1024)S(1)} %get-tuple-element.17, f32[96,2048]{1,0:T(8,128)S(1)} %bitcast_convert_fusion.3, f32[768]{0:T(1024)S(1)} %div.39, bf16[]{:T(256)} %constant.36.clone.1), kind=kCustom, calls=%fused_computation.24 | custom fusion | flops 3145728 | bytes 4198402 | tf_op jit(solution)/shard_map/scatter | solution.py:35
  23.2 4.8 reshape.280
  28.1 10.5 %all-to-all-start.2 = ((bf16[32,1,26,2048]{3,2,1,0:T(8,128)(2,1)}), bf16[32,1,26,2048]{3,2,1,0:T(8,128)(2,1)}, u32[]{:S(2)}, u32[]{:S(2)}) async-start(bf16[32,1,26,2048]{3,2,1,0:T(8,128)(2,1)} %bitcast.271), calls=%async_computation.2 | async-start | bytes 8388608 | tf_op jit(solution)/shard_map/all_to_all | solution.py:124
  38.6 9.0 %scatter_custom_fusion.2 = bf16[832,2048]{1,0:T(8,128)(2,1)} fusion(s32[768]{0:T(1024)S(1)} %get-tuple-element.17, bf16[]{:T(256)} %constant.36.clone.1, bf16[96,2048]{1,0:T(8,128)(2,1)S(1)} %bitcast.268), kind=kCustom, calls=%fused_computation.31 | custom fusion | bytes 3801090 | tf_op jit(solution)/shard_map/scatter | solution.py:35
  47.6 4.9 reshape.284
  52.4 80.0 %all-to-all-done.2 = bf16[32,1,26,2048]{3,2,1,0:T(8,128)(2,1)} async-done(((bf16[32,1,26,2048]{3,2,1,0:T(8,128)(2,1)}), bf16[32,1,26,2048]{3,2,1,0:T(8,128)(2,1)}, u32[]{:S(2)}, u32[]{:S(2)}) %all-to-all-start.2) | async-done | bytes 3407904 | tf_op jit(solution)/shard_map/all_to_all | solution.py:124
  132.5 7.5 %all-to-all-start.3 = ((bf16[32,1,26,2048]{3,2,1,0:T(8,128)(2,1)}), bf16[32,1,26,2048]{3,2,1,0:T(8,128)(2,1)}, u32[]{:S(2)}, u32[]{:S(2)}) async-start(bf16[32,1,26,2048]{3,2,1,0:T(8,128)(2,1)} %bitcast.270), calls=%async_computation.3 | async-start | bytes 8388608 | tf_op jit(solution)/shard_map/all_to_all | solution.py:123
  140.0 8.9 %scatter_custom_fusion = bf16[832,2048]{1,0:T(8,128)(2,1)} fusion(s32[768]{0:T(1024)S(1)} %get-tuple-element.16, bf16[]{:T(256)} %constant.36.clone.1, bf16[96,2048]{1,0:T(8,128)(2,1)S(1)} %bitcast.272), kind=kCustom, calls=%fused_computation.33 | custom fusion | bytes 3801090 | tf_op jit(solution)/shard_map/scatter | solution.py:35
  148.9 4.9 reshape.272
  153.8 80.2 %all-to-all-done.3 = bf16[32,1,26,2048]{3,2,1,0:T(8,128)(2,1)} async-done(((bf16[32,1,26,2048]{3,2,1,0:T(8,128)(2,1)}), bf16[32,1,26,2048]{3,2,1,0:T(8,128)(2,1)}, u32[]{:S(2)}, u32[]{:S(2)}) %all-to-all-start.3) | async-done | bytes 3407904 | tf_op jit(solution)/shard_map/all_to_all | solution.py:123
  234.1 7.6 %all-to-all-start = ((bf16[32,1,26,2048]{3,2,1,0:T(8,128)(2,1)}), bf16[32,1,26,2048]{3,2,1,0:T(8,128)(2,1)}, u32[]{:S(2)}, u32[]{:S(2)}) async-start(bf16[32,1,26,2048]{3,2,1,0:T(8,128)(2,1)} %bitcast.269), calls=%async_computation | async-start | bytes 8388608 | tf_op jit(solution)/shard_map/all_to_all | solution.py:122
  244.4 4.2 fusion.79
  248.7 4.8 fusion.74
  253.5 5.7 %multiply_convert_fusion.2 = (bf16[32,1,26,384]{3,0,2,1:T(8,128)(2,1)S(1)}, bf16[32,1,26,384]{3,0,2,1:T(8,128)(2,1)S(1)}, f32[32,1,26,384]{3,0,2,1:T(8,128)}) fusion(f32[32,1,26,384]{3,0,2,1:T(8,128)S(1)} %fusion.74, f32[32,1,26,384]{3,0,2,1:T(8,128)S(1)} %fusion.79, bf16[1,1,2048,384]{3,2,1,0:T(8,128)(2,1)S(1)} %copy-done.4, ...), kind=kOutput, calls=%fused_computation.85 | convolution fusion | flops 1312776192 | bytes 10092544 | tf_op jit(solution)/shard_map/semd,edf->semf/dot_general | solution.py:44
  264.2 21.9 %collective-permute-done.4 = bf16[1,1024,384]{2,1,0:T(8,128)(2,1)S(1)} collective-permute-done((bf16[1,1024,384]{2,1,0:T(8,128)(2,1)S(1)}, bf16[1,1024,384]{2,1,0:T(8,128)(2,1)S(1)}, u32[]{:S(2)}, u32[]{:S(2)}) %collective-permute-start.4) | collective-permute-done | bytes 786464 | tf_op jit(solution)/shard_map/ppermute | solution.py:17
  286.2 21.0 %collective-permute-done.5 = bf16[32,1,26,384]{3,0,2,1:T(8,128)(2,1)S(1)} collective-permute-done((bf16[32,1,26,384]{3,0,2,1:T(8,128)(2,1)S(1)}, bf16[32,1,26,384]{3,0,2,1:T(8,128)(2,1)S(1)}, u32[]{:S(2)}, u32[]{:S(2)}) %collective-permute-start.5) | collective-permute-done | bytes 639008 | tf_op jit(solution)/shard_map/ppermute | solution.py:17
  308.7 29.1 %collective-permute-done.2 = bf16[1,1024,384]{2,1,0:T(8,128)(2,1)S(1)} collective-permute-done((bf16[1,1024,384]{2,1,0:T(8,128)(2,1)S(1)}, bf16[1,1024,384]{2,1,0:T(8,128)(2,1)S(1)}, u32[]{:S(2)}, u32[]{:S(2)}) %collective-permute-start.2) | collective-permute-done | bytes 786464 | tf_op jit(solution)/shard_map/ppermute | solution.py:17
  337.8 13.2 %collective-permute-done.3 = bf16[32,1,26,384]{3,0,2,1:T(8,128)(2,1)S(1)} collective-permute-done((bf16[32,1,26,384]{3,0,2,1:T(8,128)(2,1)S(1)}, bf16[32,1,26,384]{3,0,2,1:T(8,128)(2,1)S(1)}, u32[]{:S(2)}, u32[]{:S(2)}) %collective-permute-start.3) | collective-permute-done | bytes 639008 | tf_op jit(solution)/shard_map/ppermute | solution.py:17
  354.9 8.4 %all-to-all-start.4 = ((bf16[32,1,26,1024]{3,2,1,0:T(8,128)(2,1)}), bf16[32,1,26,1024]{3,2,1,0:T(8,128)(2,1)S(1)}, u32[]{:S(2)}, u32[]{:S(2)}) async-start(bf16[32,1,26,1024]{3,2,1,0:T(8,128)(2,1)} %copy.48), calls=%async_computation.4 | async-start | bytes 4194304 | tf_op jit(solution)/shard_map/all_to_all | solution.py:144
  366.2 4.3 fusion.64
  370.5 4.5 fusion.94
  377.3 25.5 %collective-permute-done = bf16[1,384,1024]{2,1,0:T(8,128)(2,1)S(1)} collective-permute-done((bf16[1,384,1024]{2,1,0:T(8,128)(2,1)S(1)}, bf16[1,384,1024]{2,1,0:T(8,128)(2,1)S(1)}, u32[]{:S(2)}, u32[]{:S(2)}) %collective-permute-start) | collective-permute-done | bytes 786464 | tf_op jit(solution)/shard_map/ppermute | solution.py:17
  402.9 16.6 %collective-permute-done.1 = bf16[32,1,26,384]{3,0,2,1:T(8,128)(2,1)S(1)} collective-permute-done((bf16[32,1,26,384]{3,0,2,1:T(8,128)(2,1)S(1)}, bf16[32,1,26,384]{3,0,2,1:T(8,128)(2,1)S(1)}, u32[]{:S(2)}, u32[]{:S(2)}) %collective-permute-start.1) | collective-permute-done | bytes 639008 | tf_op jit(solution)/shard_map/ppermute | solution.py:17
  424.7 8.0 %all-to-all-start.1 = ((bf16[32,1,26,1024]{3,2,1,0:T(8,128)(2,1)}), bf16[32,1,26,1024]{3,2,1,0:T(8,128)(2,1)}, u32[]{:S(2)}, u32[]{:S(2)}) async-start(bf16[32,1,26,1024]{3,2,1,0:T(8,128)(2,1)} %copy.38), calls=%async_computation.1 | async-start | bytes 4194304 | tf_op jit(solution)/shard_map/all_to_all | solution.py:143
  432.9 6.8 %fusion.36 = bf16[1,1,2048,384]{3,2,1,0:T(8,128)(2,1)} fusion(bf16[32,1,26,2048]{3,2,1,0:T(8,128)(2,1)} %all-to-all-done.3, bf16[32,1,26,384]{3,0,2,1:T(8,128)(2,1)} %copy-done.13), kind=kOutput, calls=%fused_computation.41 | convolution fusion | flops 1309409280 | bytes 5619712 | tf_op jit(solution)/shard_map/semd,semf->edf/dot_general | solution.py:64
  439.6 6.5 %fusion.42 = bf16[1,1,384,2048]{3,2,1,0:T(8,128)(2,1)} fusion(bf16[32,1,26,2048]{3,2,1,0:T(8,128)(2,1)} %all-to-all-done.2, f32[32,1,26,384]{3,0,2,1:T(8,128)S(1)} %copy-done.15, f32[32,1,26,384]{3,0,2,1:T(8,128)S(1)} %copy-done.16), kind=kOutput, calls=%fused_computation.43 | convolution fusion | flops 1311326208 | bytes 7536640 | tf_op jit(solution)/shard_map/semf,semd->efd/dot_general | solution.py:68
  448.7 3.6 gather_fusion.1
  454.8 28.0 %all-to-all-done.1 = bf16[32,1,26,1024]{3,2,1,0:T(8,128)(2,1)} async-done(((bf16[32,1,26,1024]{3,2,1,0:T(8,128)(2,1)}), bf16[32,1,26,1024]{3,2,1,0:T(8,128)(2,1)}, u32[]{:S(2)}, u32[]{:S(2)}) %all-to-all-start.1) | async-done | bytes 1703968 | tf_op jit(solution)/shard_map/all_to_all | solution.py:143
  485.3 3.6 gather_fusion
  491.4 13.4 %all_gather.3 = bf16[192,2048]{1,0:T(8,128)(2,1)S(1)} all-gather(bf16[192,1024]{1,0:T(8,128)(2,1)S(1)} %pad_maximum_fusion), channel_id=1, replica_groups=mesh['section'=4,'expert'=32,'dp'=2] {'dp'}, dimensions={1}, use_global_device_ids=true | all-gather | bytes 1179648 | tf_op jit(solution)/shard_map/all_gather | solution.py:150
  507.9 6.5 %fusion.39 = bf16[1,1,2048,384]{3,2,1,0:T(8,128)(2,1)} fusion(bf16[32,1,26,2048]{3,2,1,0:T(8,128)(2,1)} %all-to-all-done.3, bf16[32,1,26,384]{3,0,2,1:T(8,128)(2,1)S(1)} %copy-done.12), kind=kOutput, calls=%fused_computation.42 | convolution fusion | flops 1309409280 | bytes 5619712 | tf_op jit(solution)/shard_map/semd,semf->edf/dot_general | solution.py:67
  515.5 3.6 collective-permute-done.6
  (99 shorter events, 49.3 us)
Async XLA Ops:
  0.6 37.9 %copy-start = (bf16[1,96,2048]{2,1,0:T(8,128)(2,1)S(1)}, bf16[1,96,2048]{2,1,0:T(8,128)(2,1)}, u32[]{:S(2)}) copy-start(bf16[1,96,2048]{2,1,0:T(8,128)(2,1)} %param.13) | copy-start | bytes 1179652
  0.6 9.6 %copy-start.9 = (bf16[1,96,2048]{2,1,0:T(8,128)(2,1)S(1)}, bf16[1,96,2048]{2,1,0:T(8,128)(2,1)}, u32[]{:S(2)}) copy-start(bf16[1,96,2048]{2,1,0:T(8,128)(2,1)} %param.16) | copy-start | bytes 1179652
  28.1 104.4 %all-to-all-start.2 = ((bf16[32,1,26,2048]{3,2,1,0:T(8,128)(2,1)}), bf16[32,1,26,2048]{3,2,1,0:T(8,128)(2,1)}, u32[]{:S(2)}, u32[]{:S(2)}) async-start(bf16[32,1,26,2048]{3,2,1,0:T(8,128)(2,1)} %bitcast.271), calls=%async_computation.2 | async-start | bytes 8388608 | tf_op jit(solution)/shard_map/all_to_all | solution.py:124
  132.5 7.5 %copy-start.8 = (bf16[1,96,2048]{2,1,0:T(8,128)(2,1)S(1)}, bf16[1,96,2048]{2,1,0:T(8,128)(2,1)}, u32[]{:S(2)}) copy-start(bf16[1,96,2048]{2,1,0:T(8,128)(2,1)} %param.10) | copy-start | bytes 1179652
  132.5 101.6 %all-to-all-start.3 = ((bf16[32,1,26,2048]{3,2,1,0:T(8,128)(2,1)}), bf16[32,1,26,2048]{3,2,1,0:T(8,128)(2,1)}, u32[]{:S(2)}, u32[]{:S(2)}) async-start(bf16[32,1,26,2048]{3,2,1,0:T(8,128)(2,1)} %bitcast.270), calls=%async_computation.3 | async-start | bytes 8388608 | tf_op jit(solution)/shard_map/all_to_all | solution.py:123
  234.1 7.6 %copy-start.6 = (bf16[1,1,2048,384]{3,2,1,0:T(8,128)(2,1)S(1)}, bf16[1,1,2048,384]{3,2,1,0:T(8,128)(2,1)}, u32[]{:S(2)}) copy-start(bf16[1,1,2048,384]{3,2,1,0:T(8,128)(2,1)} %param.18) | copy-start | bytes 4718596
  234.1 120.8 %all-to-all-start = ((bf16[32,1,26,2048]{3,2,1,0:T(8,128)(2,1)}), bf16[32,1,26,2048]{3,2,1,0:T(8,128)(2,1)}, u32[]{:S(2)}, u32[]{:S(2)}) async-start(bf16[32,1,26,2048]{3,2,1,0:T(8,128)(2,1)} %bitcast.269), calls=%async_computation | async-start | bytes 8388608 | tf_op jit(solution)/shard_map/all_to_all | solution.py:122
  241.8 6.8 %copy-start.3 = (bf16[1,1,384,2048]{3,2,1,0:T(8,128)(2,1)S(1)}, bf16[1,1,384,2048]{3,2,1,0:T(8,128)(2,1)}, u32[]{:S(2)}) copy-start(bf16[1,1,384,2048]{3,2,1,0:T(8,128)(2,1)} %param.19) | copy-start | bytes 4718596
  241.8 44.3 %collective-permute-start.4 = (bf16[1,1024,384]{2,1,0:T(8,128)(2,1)S(1)}, bf16[1,1024,384]{2,1,0:T(8,128)(2,1)S(1)}, u32[]{:S(2)}, u32[]{:S(2)}) collective-permute-start(bf16[1,1024,384]{2,1,0:T(8,128)(2,1)S(1)} %get-tuple-element.12), channel_id=1, source_target_pairs={{0,1},{1,0},{2,3},{3,2},{4,5},{5,4},{6,7},{7,6},{8,9},{9,8},{10,11... | collective-permute-start | bytes 2359304 | tf_op jit(solution)/shard_map/ppermute | solution.py:17
  248.7 4.8 copy-start.14
  248.7 4.8 copy-start.4
  259.2 49.4 %copy-start.11 = (bf16[32,1,26,384]{3,0,2,1:T(8,128)(2,1)}, bf16[32,1,26,384]{3,0,2,1:T(8,128)(2,1)S(1)}, u32[]{:S(2)}) copy-start(bf16[32,1,26,384]{3,0,2,1:T(8,128)(2,1)S(1)} %get-tuple-element.6) | copy-start | bytes 1916932
  259.2 91.8 %copy-start.13 = (bf16[32,1,26,384]{3,0,2,1:T(8,128)(2,1)}, bf16[32,1,26,384]{3,0,2,1:T(8,128)(2,1)S(1)}, u32[]{:S(2)}) copy-start(bf16[32,1,26,384]{3,0,2,1:T(8,128)(2,1)S(1)} %get-tuple-element.5) | copy-start | bytes 1916932
  259.2 47.9 %collective-permute-start.5 = (bf16[32,1,26,384]{3,0,2,1:T(8,128)(2,1)S(1)}, bf16[32,1,26,384]{3,0,2,1:T(8,128)(2,1)S(1)}, u32[]{:S(2)}, u32[]{:S(2)}) collective-permute-start(bf16[32,1,26,384]{3,0,2,1:T(8,128)(2,1)S(1)} %get-tuple-element.6), channel_id=1, source_target_pairs={{0,1},{1,0},{2,3},{3,2},{4,5},{5,4},{6,7},{7,6},{8,9},{9,8},{10,11... | collective-permute-start | bytes 1916936 | tf_op jit(solution)/shard_map/ppermute | solution.py:17
  260.6 77.2 %collective-permute-start.2 = (bf16[1,1024,384]{2,1,0:T(8,128)(2,1)S(1)}, bf16[1,1024,384]{2,1,0:T(8,128)(2,1)S(1)}, u32[]{:S(2)}, u32[]{:S(2)}) collective-permute-start(bf16[1,1024,384]{2,1,0:T(8,128)(2,1)S(1)} %get-tuple-element.10), channel_id=1, source_target_pairs={{0,1},{1,0},{2,3},{3,2},{4,5},{5,4},{6,7},{7,6},{8,9},{9,8},{10,11... | collective-permute-start | bytes 2359304 | tf_op jit(solution)/shard_map/ppermute | solution.py:17
  263.0 88.0 %collective-permute-start.3 = (bf16[32,1,26,384]{3,0,2,1:T(8,128)(2,1)S(1)}, bf16[32,1,26,384]{3,0,2,1:T(8,128)(2,1)S(1)}, u32[]{:S(2)}, u32[]{:S(2)}) collective-permute-start(bf16[32,1,26,384]{3,0,2,1:T(8,128)(2,1)S(1)} %get-tuple-element.5), channel_id=1, source_target_pairs={{0,1},{1,0},{2,3},{3,2},{4,5},{5,4},{6,7},{7,6},{8,9},{9,8},{10,11... | collective-permute-start | bytes 1916936 | tf_op jit(solution)/shard_map/ppermute | solution.py:17
  354.9 68.4 %all-to-all-start.4 = ((bf16[32,1,26,1024]{3,2,1,0:T(8,128)(2,1)}), bf16[32,1,26,1024]{3,2,1,0:T(8,128)(2,1)S(1)}, u32[]{:S(2)}, u32[]{:S(2)}) async-start(bf16[32,1,26,1024]{3,2,1,0:T(8,128)(2,1)} %copy.48), calls=%async_computation.4 | async-start | bytes 4194304 | tf_op jit(solution)/shard_map/all_to_all | solution.py:144
  363.2 3.0 copy-start.5
  364.9 5.6 %copy-start.7 = (bf16[1,1,2048,384]{3,2,1,0:T(8,128)(2,1)S(1)}, bf16[1,1,2048,384]{3,2,1,0:T(8,128)(2,1)}, u32[]{:S(2)}) copy-start(bf16[1,1,2048,384]{3,2,1,0:T(8,128)(2,1)} %param.18) | copy-start | bytes 4718596
  364.9 38.0 %collective-permute-start = (bf16[1,384,1024]{2,1,0:T(8,128)(2,1)S(1)}, bf16[1,384,1024]{2,1,0:T(8,128)(2,1)S(1)}, u32[]{:S(2)}, u32[]{:S(2)}) collective-permute-start(bf16[1,384,1024]{2,1,0:T(8,128)(2,1)S(1)} %get-tuple-element.8), channel_id=1, source_target_pairs={{0,1},{1,0},{2,3},{3,2},{4,5},{5,4},{6,7},{7,6},{8,9},{9,8},{10,11... | collective-permute-start | bytes 2359304 | tf_op jit(solution)/shard_map/ppermute | solution.py:17
  375.0 44.4 %collective-permute-start.1 = (bf16[32,1,26,384]{3,0,2,1:T(8,128)(2,1)S(1)}, bf16[32,1,26,384]{3,0,2,1:T(8,128)(2,1)S(1)}, u32[]{:S(2)}, u32[]{:S(2)}) collective-permute-start(bf16[32,1,26,384]{3,0,2,1:T(8,128)(2,1)S(1)} %fusion.94), channel_id=1, source_target_pairs={{0,1},{1,0},{2,3},{3,2},{4,5},{5,4},{6,7},{7,6},{8,9},{9,8},{10,11... | collective-permute-start | bytes 1916936 | tf_op jit(solution)/shard_map/ppermute | solution.py:17
  423.3 9.4 %copy-start.10 = (s32[1,96,8]{1,2,0:T(8,128)S(1)}, s32[1,96,8]{1,2,0:T(8,128)}, u32[]{:S(2)}) copy-start(s32[1,96,8]{1,2,0:T(8,128)} %param.12) | copy-start | bytes 9220
  423.3 1.4 copy-start.2
  424.7 58.2 %all-to-all-start.1 = ((bf16[32,1,26,1024]{3,2,1,0:T(8,128)(2,1)}), bf16[32,1,26,1024]{3,2,1,0:T(8,128)(2,1)}, u32[]{:S(2)}, u32[]{:S(2)}) async-start(bf16[32,1,26,1024]{3,2,1,0:T(8,128)(2,1)} %copy.38), calls=%async_computation.1 | async-start | bytes 4194304 | tf_op jit(solution)/shard_map/all_to_all | solution.py:143
  432.9 6.8 %copy-start.15 = (f32[32,1,26,384]{3,0,2,1:T(8,128)S(1)}, f32[32,1,26,384]{3,0,2,1:T(8,128)}, u32[]{:S(2)}) copy-start(f32[32,1,26,384]{3,0,2,1:T(8,128)} %copy-done.14) | copy-start | bytes 3833860
  432.9 6.8 %copy-start.16 = (f32[32,1,26,384]{3,0,2,1:T(8,128)S(1)}, f32[32,1,26,384]{3,0,2,1:T(8,128)}, u32[]{:S(2)}) copy-start(f32[32,1,26,384]{3,0,2,1:T(8,128)} %get-tuple-element.15) | copy-start | bytes 3833860
  491.4 16.5 %copy-start.12 = (bf16[32,1,26,384]{3,0,2,1:T(8,128)(2,1)S(1)}, bf16[32,1,26,384]{3,0,2,1:T(8,128)(2,1)}, u32[]{:S(2)}) copy-start(bf16[32,1,26,384]{3,0,2,1:T(8,128)(2,1)} %copy-done.11) | copy-start | bytes 1916932
  504.9 10.6 %collective-permute-start.7 = (bf16[1,96,2048]{2,1,0:T(8,128)(2,1)S(1)}, bf16[1,96,2048]{2,1,0:T(8,128)(2,1)S(1)}, u32[]{:S(2)}, u32[]{:S(2)}) collective-permute-start(bf16[1,96,2048]{2,1,0:T(8,128)(2,1)S(1)} %get-tuple-element.13), channel_id=1, source_target_pairs={{64,0},{128,64},{192,128},{0,192},{65,1},{129,65},{193,129},{1,193... | collective-permute-start | bytes 1179656 | tf_op jit(solution)/shard_map/ppermute | solution.py:13
  507.7 11.4 %collective-permute-start.6 = (bf16[1,96,2048]{2,1,0:T(8,128)(2,1)S(1)}, bf16[1,96,2048]{2,1,0:T(8,128)(2,1)S(1)}, u32[]{:S(2)}, u32[]{:S(2)}) collective-permute-start(bf16[1,96,2048]{2,1,0:T(8,128)(2,1)S(1)} %get-tuple-element.14), channel_id=1, source_target_pairs={{192,0},{0,64},{64,128},{128,192},{193,1},{1,65},{65,129},{129,193... | collective-permute-start | bytes 1179656 | tf_op jit(solution)/shard_map/ppermute | solution.py:13
  507.9 12.6 %copy-start.1 = (bf16[1,96,2048]{2,1,0:T(8,128)(2,1)S(1)}, bf16[1,96,2048]{2,1,0:T(8,128)(2,1)}, u32[]{:S(2)}) copy-start(bf16[1,96,2048]{2,1,0:T(8,128)(2,1)} %param.13) | copy-start | bytes 1179652
